TPU v7x, 32 devices: a whole 2x2x4 slice. The times are simulated.
32 devices in a mesh: fsdp: 8 (over y, x, core), win: 4 (over z).
Axes of the slice: x: 2, y: 2, z: 4, core: 2. Of those that a mesh axis runs over, the one named last changes fastest.
Arguments:
- tokens: bfloat16 [16384, 2048], P(('fsdp', 'win')), may hold values from -16 to 16
- block_map: int32 [8, 4], P('fsdp'), may hold values from 0 to 3, each once within a row
- shift: int32 [8], P('fsdp'), may hold values from 1 to 2047
- ln_gain: float32 [2048], replicated, may hold values from 0.5 to 1.5
- w_query: bfloat16 [2048, 1024], P('fsdp'), may hold values from -1 to 1
- w_key: bfloat16 [2048, 1024], P('fsdp'), may hold values from -1 to 1
- w_value: bfloat16 [2048, 1024], P('fsdp'), may hold values from -0.125 to 0.125
- w_out: bfloat16 [1024, 2048], P('fsdp'), may hold values from -0.1875 to 0.1875
- logit_scale: float32 [16], replicated, may hold values from 1 to 300
Outputs:
- mixed: bfloat16 [16384, 2048], P(('fsdp', 'win'))
All inputs are finite; a program needn't handle non-finite values.
Results may differ from a plain program's by a relative error of at most 0.008.
Values may be sent and summed in bfloat16 or wider, within the bound.
A program may use at most 128 MiB of HBM per device.

v0:
```python
import jax
import jax.numpy as jnp
from jax import lax
from jax.sharding import PartitionSpec as P


def layer_norm(resid, gain):
    center = jnp.mean(resid, axis=-1, keepdims=True)
    centred = resid - center
    spread = jnp.mean(centred * centred, axis=-1, keepdims=True)
    return (centred * lax.rsqrt(spread + 1e-05) * gain).astype(jnp.bfloat16)


def unit_heads(values, head_count):
    split = values.reshape(values.shape[0], head_count, -1)
    scale = lax.rsqrt(jnp.sum(split * split, axis=-1, keepdims=True) + 1e-06)
    return (split * scale).astype(jnp.bfloat16)


def block_length():
    return 512


def per_device(tokens, block_map, shift, ln_gain, w_query, w_key, w_value, w_out, logit_scale):
    tok_rows = tokens.shape[0]
    head_count = logit_scale.shape[0]
    inner = w_query.shape[1]
    head_size = inner // head_count
    groups = lax.axis_size("win")
    member = lax.axis_index("win")
    block_row = block_map[0]
    offset = shift[0]
    resid = tokens.astype(jnp.float32)
    normed = layer_norm(resid, ln_gain)
    group_ids = jnp.arange(groups, dtype=jnp.int32)

    def region_of(index):
        owner = index // tok_rows
        picked = owner[:, None] == group_ids[None, :]
        block = jnp.sum(jnp.where(picked, block_row[None, :], 0), axis=1)
        return block * tok_rows + index % tok_rows >= offset

    pieces = (
        lax.all_gather(w_query, "fsdp", axis=0, tiled=True),
        lax.all_gather(w_key, "fsdp", axis=0, tiled=True),
        lax.all_gather(w_value, "fsdp", axis=0, tiled=True),
    )
    columns = normed
    query, key_full, value = tuple(
        (jnp.dot(columns, piece, preferred_element_type=jnp.float32) for piece in pieces)
    )
    q_unit = unit_heads(query, head_count)
    k_flat = unit_heads(key_full, head_count).reshape(tok_rows, inner)
    value_half = value.astype(jnp.bfloat16)
    own_region = region_of(member * tok_rows + jnp.arange(tok_rows, dtype=jnp.int32))
    start_state = (
        jnp.full((head_count, tok_rows), -1e30, jnp.float32),
        jnp.zeros((head_count, tok_rows), jnp.float32),
        jnp.zeros((tok_rows, head_count, head_size), jnp.float32),
    )

    def attend_block(carry, packed):
        best, total, accum = carry
        keys, values, regions = packed
        allowed = (own_region[:, None] == regions[None, :])[None]
        score = (
            jnp.einsum("ihd,jhd->hij", q_unit, keys, preferred_element_type=jnp.float32)
            * logit_scale[:, None, None]
        )
        score = jnp.where(allowed, score, -1e30)
        new_best = jnp.maximum(best, jnp.max(score, axis=-1))
        weight = jnp.where(allowed, jnp.exp(score - new_best[:, :, None]), 0.0)
        fade = jnp.exp(best - new_best)
        total = total * fade + jnp.sum(weight, axis=-1)
        accum = accum * fade.T[:, :, None] + jnp.einsum(
            "hij,jhd->ihd", weight.astype(jnp.bfloat16), values, preferred_element_type=jnp.float32
        )
        return ((new_best, total, accum), None)

    carry = start_state
    pieces = (
        lax.all_gather(k_flat, "win", axis=0, tiled=True),
        lax.all_gather(value_half, "win", axis=0, tiled=True),
    )
    count = pieces[0].shape[0]
    blk = block_length()
    nblk = count // blk
    keys = pieces[0].reshape(nblk, blk, head_count, head_size)
    values = pieces[1].reshape(nblk, blk, head_count, head_size)
    regions = region_of(jnp.arange(count, dtype=jnp.int32)).reshape(nblk, blk)
    carry, unused = lax.scan(attend_block, carry, (keys, values, regions))
    best, total, accum = carry
    attended = (accum / total.T[:, :, None]).reshape(tok_rows, inner).astype(jnp.bfloat16)
    columns = attended
    output_sum = jnp.dot(
        columns,
        lax.all_gather(w_out, "fsdp", axis=0, tiled=True),
        preferred_element_type=jnp.float32,
    )
    return (resid + output_sum).astype(jnp.bfloat16)


def solution(mesh):
    return jax.shard_map(
        per_device,
        mesh=mesh,
        in_specs=(
            P(("fsdp", "win"), None),
            P("fsdp", None),
            P("fsdp"),
            P(),
            P("fsdp", None),
            P("fsdp", None),
            P("fsdp", None),
            P("fsdp", None),
            P(),
        ),
        out_specs=P(("fsdp", "win"), None),
        check_vma=False,
    )
```

profile of v0, /device:TPU:0, one launch (start us, length us, event | category | flops | bytes accessed | tf_op | source)
XLA Modules:
  0.0 430.1 jit_solution(9494824374934924594)
XLA Ops:
  11.4 37.3 %all-gather.7.cloned.1.call-done = bf16[2048,1024]{1,0:T(8,128)(2,1)} async-done(((bf16[256,1024]{1,0:T(8,128)(2,1)}), bf16[2048,1024]{1,0:T(8,128)(2,1)}) %all-gather.7.cloned.1.call-update) | async-done | bytes 4194320 | tf_op jit(solution)/shard_map/all_gather | solution.py:45
  48.7 6.6 %fusion.41 = (f32[512,1024]{1,0:T(8,128)}, f32[512,1024]{1,0:T(8,128)}) fusion(bf16[2048,1024]{1,0:T(8,128)(2,1)} %all-gather.7.cloned.1.call-done, bf16[512,2048]{1,0:T(8,128)(2,1)S(1)} %copy-done.1, f32[2048]{0:T(1024)S(1)} %copy-done.4, f32[512]{0:T(512)S(1)} %add_rsqrt_fusion.2, f32[512]{0:T(512)S(1)} %broadcast_multiply_fusion.1), kind=kOutput, calls=%fused_computation.76 | convolution fusion | flops 2153250816 | bytes 10498048 | tf_op jit(solution)/shard_map/dot_general | solution.py:50
  68.4 18.9 %all-gather.13.cloned.1.call-done = bf16[2048,1024]{1,0:T(8,128)(2,1)} async-done(((bf16[256,1024]{1,0:T(8,128)(2,1)}), bf16[2048,1024]{1,0:T(8,128)(2,1)}) %all-gather.13.cloned.1.call-update) | async-done | bytes 4194320 | tf_op jit(solution)/shard_map/all_gather | solution.py:46
  87.3 5.6 %convolution_convert_fusion = bf16[512,1024]{1,0:T(8,128)(2,1)} fusion(bf16[2048,1024]{1,0:T(8,128)(2,1)} %all-gather.13.cloned.1.call-done, bf16[512,2048]{1,0:T(8,128)(2,1)S(1)} %copy-done.1, f32[2048]{0:T(1024)S(1)} %copy-done.4, f32[512]{0:T(512)S(1)} %add_rsqrt_fusion.2, f32[512]{0:T(512)S(1)} %broadcast_multiply_fusion.1), kind=kOutput, calls=%fused_computation.39 | convolution fusion | flops 2153250816 | bytes 7352320 | tf_op jit(solution)/shard_map/dot_general | solution.py:50
  94.5 31.4 %all-gather.11.cloned.1.call-done = bf16[2048,1024]{1,0:T(8,128)(2,1)} async-done(((bf16[256,1024]{1,0:T(8,128)(2,1)}), bf16[2048,1024]{1,0:T(8,128)(2,1)}) %all-gather.11.cloned.1.call-update) | async-done | bytes 4194320 | tf_op jit(solution)/shard_map/all_gather | solution.py:44
  126.0 4.7 %multiply_reduce_fusion = (f32[512,16]{0,1:T(8,128)S(1)}, f32[512,1024]{0,1:T(8,128)S(1)}) fusion(bf16[2048,1024]{1,0:T(8,128)(2,1)} %all-gather.11.cloned.1.call-done, bf16[512,2048]{1,0:T(8,128)(2,1)S(1)} %copy-done.1, f32[2048]{0:T(1024)S(1)} %copy-done.4, f32[512]{0:T(512)S(1)} %add_rsqrt_fusion.2, f32[512]{0:T(512)S(1)} %broadcast_multiply_fusion.1), kind=kOutput, calls=%fused_computation.37 | convolution fusion | flops 2153766912 | bytes 8433664 | tf_op jit(solution)/shard_map/dot_general | solution.py:50
  131.1 77.1 %all-gather.9.cloned.1.call-done = bf16[2048,1024]{1,0:T(8,128)(2,1)} async-done(((bf16[512,1024]{1,0:T(8,128)(2,1)}), bf16[2048,1024]{1,0:T(8,128)(2,1)}) %all-gather.9.cloned.1.call-update) | async-done | bytes 4194320 | tf_op jit(solution)/shard_map/all_gather | solution.py:82
  208.2 11.8 %reshape.112 = bf16[4,512,16,64]{3,2,1,0:T(8,128)(2,1)} reshape(bf16[2048,1024]{1,0:T(8,128)(2,1)} %all-gather.9.cloned.1.call-done) | data formatting | bytes 8388608 | tf_op jit(solution)/shard_map/reshape | solution.py:88
  220.0 9.8 %copy.29 = bf16[4,512,16,64]{1,3,2,0:T(8,128)(2,1)} copy(bf16[4,512,16,64]{3,2,1,0:T(8,128)(2,1)} %reshape.112) | data formatting | bytes 8388608
  229.8 59.2 %all-gather.15.cloned.1.call-done = bf16[2048,1024]{1,0:T(8,128)(2,1)} async-done(((bf16[512,1024]{1,0:T(8,128)(2,1)}), bf16[2048,1024]{1,0:T(8,128)(2,1)}) %all-gather.15.cloned.1.call-update) | async-done | bytes 4194320 | tf_op jit(solution)/shard_map/all_gather | solution.py:83
  288.9 11.7 %reshape.113 = bf16[4,512,16,64]{3,2,1,0:T(8,128)(2,1)} reshape(bf16[2048,1024]{1,0:T(8,128)(2,1)} %all-gather.15.cloned.1.call-done) | data formatting | bytes 8388608 | tf_op jit(solution)/shard_map/reshape | solution.py:89
  300.6 9.8 %copy.30 = bf16[4,512,16,64]{1,3,2,0:T(8,128)(2,1)} copy(bf16[4,512,16,64]{3,2,1,0:T(8,128)(2,1)} %reshape.113) | data formatting | bytes 8388608
  310.4 105.1 %while.15 = (s32[]{:T(128)}, f32[16,512]{1,0:T(8,128)S(1)}, f32[16,512]{1,0:T(8,128)S(1)}, f32[512,16,64]{0,2,1:T(8,128)}, pred[512]{0:T(512)(128)(4,1)S(1)}, /*...) while((s32[]{:T(128)}, f32[16,512]{1,0:T(8,128)S(1)}, ...), condition=%wide.region_9.10_spmd.clone, body=%wide.region_6.9_spmd.clone.sunk | while | flops 1130151936 | bytes 126356832 | solution.py:91
  310.6 9.1 %fusion.58 = (f32[16,512]{1,0:T(8,128)S(1)}, f32[16,512,512]{2,1,0:T(8,128)}) fusion(f32[16]{0:T(128)S(1)} %get-tuple-element.252, pred[512,512]{0,1:T(8,128)(4,1)S(1)} %broadcast_compare_fusion.2, bf16[512,16,64]{0,2,1:T(8,128)(2,1)S(1)} %get-tuple-element.251, bf16[4,512,16,64]{1,3,2,0:T(8,128)(2,1)} %get-tuple-element.250, s32[]{:T(128)} %get-tuple-element.232), kind=kOutput, calls=%fused_computation.2.clone.1 | convolution fusion | flops 549445632 | bytes 19169856 | tf_op jit(solution)/shard_map/while/body/eval_jaxpr/ihd,jhd->hij/dot_general | solution.py:67
  319.7 12.5 %bitcast_add_fusion.2 = f32[512,16,64]{0,2,1:T(8,128)} fusion(f32[512,16,64]{0,2,1:T(8,128)} %get-tuple-element.235, f32[16,512,512]{2,1,0:T(8,128)} %get-tuple-element.218, f32[16,512]{1,0:T(8,128)S(1)} %get-tuple-element.245, f32[16]{0:T(128)S(1)} %get-tuple-element.252, pred[512,512]{0,1:T(8,128)(4,1)S(1)} %broadcast_compare_fusion.2, ...), kind=kOutput, calls=%fused_computation.7.clone.1 | convolution fusion | flops 559415296 | bytes 22348352 | tf_op jit(solution)/shard_map/while/body/eval_jaxpr/hij,jhd->ihd/dot_general | solution.py:75
  332.2 4.2 fusion.60
  336.7 8.8 %fusion.58 = (f32[16,512]{1,0:T(8,128)S(1)}, f32[16,512,512]{2,1,0:T(8,128)}) fusion(f32[16]{0:T(128)S(1)} %get-tuple-element.252, pred[512,512]{0,1:T(8,128)(4,1)S(1)} %broadcast_compare_fusion.2, bf16[512,16,64]{0,2,1:T(8,128)(2,1)S(1)} %get-tuple-element.251, bf16[4,512,16,64]{1,3,2,0:T(8,128)(2,1)} %get-tuple-element.250, s32[]{:T(128)} %get-tuple-element.232), kind=kOutput, calls=%fused_computation.2.clone.1 | convolution fusion | flops 549445632 | bytes 19169856 | tf_op jit(solution)/shard_map/while/body/eval_jaxpr/ihd,jhd->hij/dot_general | solution.py:67
  345.6 12.9 %bitcast_add_fusion.2 = f32[512,16,64]{0,2,1:T(8,128)} fusion(f32[512,16,64]{0,2,1:T(8,128)} %get-tuple-element.235, f32[16,512,512]{2,1,0:T(8,128)} %get-tuple-element.218, f32[16,512]{1,0:T(8,128)S(1)} %get-tuple-element.245, f32[16]{0:T(128)S(1)} %get-tuple-element.252, pred[512,512]{0,1:T(8,128)(4,1)S(1)} %broadcast_compare_fusion.2, ...), kind=kOutput, calls=%fused_computation.7.clone.1 | convolution fusion | flops 559415296 | bytes 22348352 | tf_op jit(solution)/shard_map/while/body/eval_jaxpr/hij,jhd->ihd/dot_general | solution.py:75
  358.4 4.2 fusion.60
  363.0 8.8 %fusion.58 = (f32[16,512]{1,0:T(8,128)S(1)}, f32[16,512,512]{2,1,0:T(8,128)}) fusion(f32[16]{0:T(128)S(1)} %get-tuple-element.252, pred[512,512]{0,1:T(8,128)(4,1)S(1)} %broadcast_compare_fusion.2, bf16[512,16,64]{0,2,1:T(8,128)(2,1)S(1)} %get-tuple-element.251, bf16[4,512,16,64]{1,3,2,0:T(8,128)(2,1)} %get-tuple-element.250, s32[]{:T(128)} %get-tuple-element.232), kind=kOutput, calls=%fused_computation.2.clone.1 | convolution fusion | flops 549445632 | bytes 19169856 | tf_op jit(solution)/shard_map/while/body/eval_jaxpr/ihd,jhd->hij/dot_general | solution.py:67
  371.8 12.9 %bitcast_add_fusion.2 = f32[512,16,64]{0,2,1:T(8,128)} fusion(f32[512,16,64]{0,2,1:T(8,128)} %get-tuple-element.235, f32[16,512,512]{2,1,0:T(8,128)} %get-tuple-element.218, f32[16,512]{1,0:T(8,128)S(1)} %get-tuple-element.245, f32[16]{0:T(128)S(1)} %get-tuple-element.252, pred[512,512]{0,1:T(8,128)(4,1)S(1)} %broadcast_compare_fusion.2, ...), kind=kOutput, calls=%fused_computation.7.clone.1 | convolution fusion | flops 559415296 | bytes 22348352 | tf_op jit(solution)/shard_map/while/body/eval_jaxpr/hij,jhd->ihd/dot_general | solution.py:75
  389.2 8.8 %fusion.58 = (f32[16,512]{1,0:T(8,128)S(1)}, f32[16,512,512]{2,1,0:T(8,128)}) fusion(f32[16]{0:T(128)S(1)} %get-tuple-element.252, pred[512,512]{0,1:T(8,128)(4,1)S(1)} %broadcast_compare_fusion.2, bf16[512,16,64]{0,2,1:T(8,128)(2,1)S(1)} %get-tuple-element.251, bf16[4,512,16,64]{1,3,2,0:T(8,128)(2,1)} %get-tuple-element.250, s32[]{:T(128)} %get-tuple-element.232), kind=kOutput, calls=%fused_computation.2.clone.1 | convolution fusion | flops 549445632 | bytes 19169856 | tf_op jit(solution)/shard_map/while/body/eval_jaxpr/ihd,jhd->hij/dot_general | solution.py:67
  398.1 12.9 %bitcast_add_fusion.2 = f32[512,16,64]{0,2,1:T(8,128)} fusion(f32[512,16,64]{0,2,1:T(8,128)} %get-tuple-element.235, f32[16,512,512]{2,1,0:T(8,128)} %get-tuple-element.218, f32[16,512]{1,0:T(8,128)S(1)} %get-tuple-element.245, f32[16]{0:T(128)S(1)} %get-tuple-element.252, pred[512,512]{0,1:T(8,128)(4,1)S(1)} %broadcast_compare_fusion.2, ...), kind=kOutput, calls=%fused_computation.7.clone.1 | convolution fusion | flops 559415296 | bytes 22348352 | tf_op jit(solution)/shard_map/while/body/eval_jaxpr/hij,jhd->ihd/dot_general | solution.py:75
  417.3 5.9 %fusion.24 = bf16[512,2048]{1,0:T(8,128)(2,1)} fusion(bf16[512,2048]{1,0:T(8,128)(2,1)S(1)} %copy-done.1, bf16[512,1024]{0,1:T(8,128)(2,1)S(1)} %bitcast.60, bf16[1024,2048]{1,0:T(8,128)(2,1)} %all-gather.17.cloned.1.call-done), kind=kOutput, calls=%fused_computation.33 | convolution fusion | flops 2150629376 | bytes 9437184 | tf_op jit(solution)/shard_map/dot_general | solution.py:95
  (75 shorter events, 30.5 us)
Async XLA Ops:
  6.5 4.2 copy-start.1
  6.5 42.2 %copy-start.4 = (f32[2048]{0:T(1024)S(1)}, f32[2048]{0:T(1024)}, u32[]{:S(2)}) copy-start(f32[2048]{0:T(1024)} %param.14) | copy-start | bytes 24580
  6.5 42.2 %all-gather.7.cloned.1.call-start = ((), (), s32[]{:S(2)}) async-start(), calls=%async_computation | async-start | bytes 4718592 | tf_op jit(solution)/shard_map/all_gather | solution.py:45
  7.3 80.1 %all-gather.13.cloned.1.call-start = ((), (), s32[]{:S(2)}) async-start(), calls=%async_computation.3 | async-start | bytes 4718592 | tf_op jit(solution)/shard_map/all_gather | solution.py:46
  8.0 118.0 %all-gather.11.cloned.1.call-start = ((), (), s32[]{:S(2)}) async-start(), calls=%async_computation.2 | async-start | bytes 4718592 | tf_op jit(solution)/shard_map/all_gather | solution.py:44
  8.7 199.5 %all-gather.9.cloned.1.call-start = ((), (), s32[]{:S(2)}) async-start(), calls=%async_computation.1 | async-start | bytes 5242880 | tf_op jit(solution)/shard_map/all_gather | solution.py:82
  68.3 25.9 %copy-start.3 = (s32[1,4]{1,0:T(1,128)S(1)}, s32[1,4]{1,0:T(1,128)}, u32[]{:S(2)}) copy-start(s32[1,4]{1,0:T(1,128)} %param.12) | copy-start | bytes 52
  68.4 220.6 %all-gather.15.cloned.1.call-start = ((), (), s32[]{:S(2)}) async-start(), calls=%async_computation.4 | async-start | bytes 5242880 | tf_op jit(solution)/shard_map/all_gather | solution.py:83
  93.0 324.4 %all-gather.17.cloned.1.call-start = ((), (), s32[]{:S(2)}) async-start(), calls=%async_computation.5 | async-start | bytes 4718592 | tf_op jit(solution)/shard_map/all_gather | solution.py:97
  300.6 9.8 %copy-start.2 = (f32[16]{0:T(128)S(1)}, f32[16]{0:T(128)}, u32[]{:S(2)}) copy-start(f32[16]{0:T(128)} %param.19) | copy-start | bytes 196
  319.7 12.5 %copy-start = (f32[16,512,512]{2,1,0:T(8,128)S(1)}, f32[16,512,512]{2,1,0:T(8,128)}, u32[]{:S(2)}) copy-start(f32[16,512,512]{2,1,0:T(8,128)} %get-tuple-element.218) | copy-start | bytes 50331652 | tf_op jit(solution)/shard_map/while
  345.6 12.9 %copy-start = (f32[16,512,512]{2,1,0:T(8,128)S(1)}, f32[16,512,512]{2,1,0:T(8,128)}, u32[]{:S(2)}) copy-start(f32[16,512,512]{2,1,0:T(8,128)} %get-tuple-element.218) | copy-start | bytes 50331652 | tf_op jit(solution)/shard_map/while
  371.8 12.9 %copy-start = (f32[16,512,512]{2,1,0:T(8,128)S(1)}, f32[16,512,512]{2,1,0:T(8,128)}, u32[]{:S(2)}) copy-start(f32[16,512,512]{2,1,0:T(8,128)} %get-tuple-element.218) | copy-start | bytes 50331652 | tf_op jit(solution)/shard_map/while
  398.1 12.9 %copy-start = (f32[16,512,512]{2,1,0:T(8,128)S(1)}, f32[16,512,512]{2,1,0:T(8,128)}, u32[]{:S(2)}) copy-start(f32[16,512,512]{2,1,0:T(8,128)} %get-tuple-element.218) | copy-start | bytes 50331652 | tf_op jit(solution)/shard_map/while
Sparse Core Ops, SparseCore 0:
  9.2 39.4 all-gather.6
  50.6 36.7 all-gather.12
  89.2 36.7 all-gather.10
  127.4 80.7 all-gather.8
  209.6 79.2 all-gather.14
  290.7 35.2 all-gather.16
where the time goes:
time: 432 us; the launch traced here: 430 us
  waiting for transfers between devices  227 us (53%)
  matrix products  109 us (25%)
  local copies, waits for them, and re-layouts  50.6 us (12%)
  other arithmetic  28.5 us (7%)
  between operations  14.3 us (3%)
    all_gather x1, waiting for transfers between devices, per_device(): lax.all_gather(k_flat, 'win', axis=0, tiled=True)  77.1 us
    all_gather x1, waiting for transfers between devices, per_device(): lax.all_gather(value_half, 'win', axis=0, tiled=True)  59.2 us
    dot_general x4, matrix products, attend_block(): jnp.einsum('hij,jhd->ihd', weight.astype(jnp.bfloat16), values, preferred...  51.1 us
    all_gather x1, waiting for transfers between devices, per_device(): lax.all_gather(w_key, 'fsdp', axis=0, tiled=True)  37.3 us
    dot_general x4, matrix products, attend_block(): jnp.einsum('ihd,jhd->hij', q_unit, keys, preferred_element_type=jnp.float32)  35.6 us
    all_gather x1, waiting for transfers between devices, per_device(): lax.all_gather(w_query, 'fsdp', axis=0, tiled=True)  31.4 us
    unnamed x10, local copies, waits for them, and re-layouts  19.5 us
    all_gather x1, waiting for transfers between devices, per_device(): lax.all_gather(w_value, 'fsdp', axis=0, tiled=True)  18.9 us
  transfers between devices with their start and end apart: 6, of which 5 were waited for; matrix products, arithmetic and copies ran while one was open for 42% of the time, Pallas kernels for 0%

commit v1 on v0

--- a/solution.py
+++ b/solution.py
@@ -2,6 +2,25 @@
 import jax.numpy as jnp
 from jax import lax
 from jax.sharding import PartitionSpec as P
+
+
+def ring_gather(x, axis, dim):
+    peers, mine, rows = (lax.axis_size(axis), lax.axis_index(axis), x.shape[dim])
+    ahead = [(i, (i + 1) % peers) for i in range(peers)]
+    left = [(i, (i - 1) % peers) for i in range(peers)]
+    out = jnp.zeros((*x.shape[:dim], peers * rows, *x.shape[dim + 1 :]), x.dtype)
+    out = lax.dynamic_update_slice_in_dim(out, x, mine * rows, axis=dim)
+    from_left = from_right = x
+    half = peers // 2
+    for hop in range(1, half + 1):
+        from_left = lax.ppermute(from_left, axis, ahead)
+        out = lax.dynamic_update_slice_in_dim(out, from_left, (mine - hop) % peers * rows, axis=dim)
+        if hop < peers - half:
+            from_right = lax.ppermute(from_right, axis, left)
+            out = lax.dynamic_update_slice_in_dim(
+                out, from_right, (mine + hop) % peers * rows, axis=dim
+            )
+    return out
 
 
 def layer_norm(resid, gain):
@@ -78,10 +97,7 @@
         return ((new_best, total, accum), None)
 
     carry = start_state
-    pieces = (
-        lax.all_gather(k_flat, "win", axis=0, tiled=True),
-        lax.all_gather(value_half, "win", axis=0, tiled=True),
-    )
+    pieces = (lax.all_gather(k_flat, "win", axis=0, tiled=True), ring_gather(value_half, "win", 0))
     count = pieces[0].shape[0]
     blk = block_length()
     nblk = count // blk

time: 432 us -> 375 us (0.87)
  waiting for transfers between devices: 227 us -> 157 us
  local copies, waits for them, and re-layouts: 50.6 us -> 60 us
    ppermute x0 -> x3, waiting for transfers between devices: none -> 68.4 us  [the longest x2 52.6 us: ring_gather(): from_left = lax.ppermute(from_left, axis, ahead)]
    all_gather x1 -> x0, waiting for transfers between devices: 59.2 us -> none  [per_device(): lax.all_gather(value_half, 'win', axis=0, tiled=True)]
    all_gather x1, waiting for transfers between devices: 77.1 us -> 24.8 us  [per_device(): lax.all_gather(k_flat, 'win', axis=0, tiled=True)]
    all_gather x1, waiting for transfers between devices: 31.4 us -> 4.92 us  [per_device(): lax.all_gather(w_query, 'fsdp', axis=0, tiled=True)]
    dynamic_update_slice x0 -> x4, local copies, waits for them, and re-layouts: none -> 7.13 us  [the longest x2 4.65 us: ring_gather(): lax.dynamic_update_slice_in_dim(out, from_left, (mine - hop) % peers * ro...]
    ppermute x0 -> x3, local copies, waits for them, and re-layouts: none -> 6.91 us  [the longest x2 4.64 us: ring_gather(): from_left = lax.ppermute(from_left, axis, ahead)]
    unnamed x10 -> x14, local copies, waits for them, and re-layouts: 19.5 us -> 16.8 us
  transfers between devices with their start and end apart: 6 -> 8, of which waited for: 5 -> 7; matrix products, arithmetic and copies ran while one was open for 42% -> 51% of each run, Pallas kernels for 0% -> 0%
where the time goes in v1:
time: 375 us; the launch traced here: 374 us
  waiting for transfers between devices  157 us (42%)
  matrix products  111 us (30%)
  local copies, waits for them, and re-layouts  60 us (16%)
  other arithmetic  28.5 us (8%)
  between operations  14 us (4%)
  starting transfers between devices  4.04 us (1%)
    ppermute x2, waiting for transfers between devices, ring_gather(): from_left = lax.ppermute(from_left, axis, ahead)  52.6 us
    dot_general x4, matrix products, attend_block(): jnp.einsum('hij,jhd->ihd', weight.astype(jnp.bfloat16), values, preferred...  51.1 us
    all_gather x1, waiting for transfers between devices, per_device(): lax.all_gather(w_key, 'fsdp', axis=0, tiled=True)  37.3 us
    dot_general x4, matrix products, attend_block(): jnp.einsum('ihd,jhd->hij', q_unit, keys, preferred_element_type=jnp.float32)  35.4 us
    all_gather x1, waiting for transfers between devices, per_device(): lax.all_gather(k_flat, 'win', axis=0, tiled=True)  24.8 us
    all_gather x1, waiting for transfers between devices, per_device(): lax.all_gather(w_value, 'fsdp', axis=0, tiled=True)  18.5 us
    dot_general x3, matrix products, per_device(): jnp.dot(columns, piece, preferred_element_type=jnp.float32)  18.2 us
    unnamed x14, local copies, waits for them, and re-layouts  16.8 us
  transfers between devices with their start and end apart: 8, of which 7 were waited for; matrix products, arithmetic and copies ran while one was open for 51% of the time, Pallas kernels for 0%

profile of v1, /device:TPU:0, one launch (start us, length us, event | category | flops | bytes accessed | tf_op | source)
XLA Modules:
  0.0 373.8 jit_solution(5075209497078917976)
XLA Ops:
  11.4 37.3 %all-gather.6.cloned.1.call-done = bf16[2048,1024]{1,0:T(8,128)(2,1)} async-done(((bf16[256,1024]{1,0:T(8,128)(2,1)}), bf16[2048,1024]{1,0:T(8,128)(2,1)}) %all-gather.6.cloned.1.call-update) | async-done | bytes 4194320 | tf_op jit(solution)/shard_map/all_gather | solution.py:64
  48.7 6.6 %fusion.41 = (f32[512,1024]{1,0:T(8,128)}, f32[512,1024]{1,0:T(8,128)}) fusion(bf16[2048,1024]{1,0:T(8,128)(2,1)} %all-gather.6.cloned.1.call-done, bf16[512,2048]{1,0:T(8,128)(2,1)S(1)} %copy-done.1, f32[2048]{0:T(1024)S(1)} %copy-done.6, f32[512]{0:T(512)S(1)} %add_rsqrt_fusion.2, f32[512]{0:T(512)S(1)} %broadcast_multiply_fusion.1), kind=kOutput, calls=%fused_computation.80 | convolution fusion | flops 2153250816 | bytes 10498048 | tf_op jit(solution)/shard_map/dot_general | solution.py:69
  68.9 18.5 %all-gather.12.cloned.1.call-done = bf16[2048,1024]{1,0:T(8,128)(2,1)} async-done(((bf16[256,1024]{1,0:T(8,128)(2,1)}), bf16[2048,1024]{1,0:T(8,128)(2,1)}) %all-gather.12.cloned.1.call-update) | async-done | bytes 4194320 | tf_op jit(solution)/shard_map/all_gather | solution.py:65
  87.3 5.6 %convolution_convert_fusion = bf16[512,1024]{1,0:T(8,128)(2,1)} fusion(bf16[2048,1024]{1,0:T(8,128)(2,1)} %all-gather.12.cloned.1.call-done, bf16[512,2048]{1,0:T(8,128)(2,1)S(1)} %copy-done.1, f32[2048]{0:T(1024)S(1)} %copy-done.6, f32[512]{0:T(512)S(1)} %add_rsqrt_fusion.2, f32[512]{0:T(512)S(1)} %broadcast_multiply_fusion.1), kind=kOutput, calls=%fused_computation.39 | convolution fusion | flops 2153250816 | bytes 7352320 | tf_op jit(solution)/shard_map/dot_general | solution.py:69
  97.7 23.3 %collective-permute-done = bf16[512,1024]{1,0:T(8,128)(2,1)} collective-permute-done((bf16[512,1024]{1,0:T(8,128)(2,1)}, bf16[512,1024]{1,0:T(8,128)(2,1)}, u32[]{:S(2)}, u32[]{:S(2)}) %collective-permute-start) | collective-permute-done | bytes 1048608 | tf_op jit(solution)/shard_map/ppermute | solution.py:16
  121.1 4.9 %all-gather.10.cloned.1.call-done = bf16[2048,1024]{1,0:T(8,128)(2,1)} async-done(((bf16[256,1024]{1,0:T(8,128)(2,1)}), bf16[2048,1024]{1,0:T(8,128)(2,1)}) %all-gather.10.cloned.1.call-update) | async-done | bytes 4194320 | tf_op jit(solution)/shard_map/all_gather | solution.py:63
  126.0 6.1 %multiply_reduce_fusion = (f32[512,16]{0,1:T(8,128)S(1)}, f32[512,1024]{0,1:T(8,128)}) fusion(bf16[2048,1024]{1,0:T(8,128)(2,1)} %all-gather.10.cloned.1.call-done, bf16[512,2048]{1,0:T(8,128)(2,1)S(1)} %copy-done.1, f32[2048]{0:T(1024)S(1)} %copy-done.6, f32[512]{0:T(512)S(1)} %add_rsqrt_fusion.2, f32[512]{0:T(512)S(1)} %broadcast_multiply_fusion.1), kind=kOutput, calls=%fused_computation.37 | convolution fusion | flops 2153766912 | bytes 8433664 | tf_op jit(solution)/shard_map/dot_general | solution.py:69
  138.9 15.8 %collective-permute-done.1 = bf16[512,1024]{1,0:T(8,128)(2,1)} collective-permute-done((bf16[512,1024]{1,0:T(8,128)(2,1)}, bf16[512,1024]{1,0:T(8,128)(2,1)}, u32[]{:S(2)}, u32[]{:S(2)}) %collective-permute-start.1) | collective-permute-done | bytes 1048608 | tf_op jit(solution)/shard_map/ppermute | solution.py:19
  161.5 29.3 %collective-permute-done.2 = bf16[512,1024]{1,0:T(8,128)(2,1)} collective-permute-done((bf16[512,1024]{1,0:T(8,128)(2,1)}, bf16[512,1024]{1,0:T(8,128)(2,1)}, u32[]{:S(2)}, u32[]{:S(2)}) %collective-permute-start.2) | collective-permute-done | bytes 1048608 | tf_op jit(solution)/shard_map/ppermute | solution.py:16
  195.4 7.8 %reshape.111 = bf16[4,512,16,64]{1,0,3,2:T(4,128)(2,1)} reshape(bf16[2048,1024]{0,1:T(8,128)(2,1)} %constant_dynamic-update-slice_fusion.3) | data formatting | bytes 8388608 | tf_op jit(solution)/shard_map/reshape | solution.py:105
  203.3 5.2 %copy.35 = bf16[4,512,16,64]{1,3,2,0:T(8,128)(2,1)} copy(bf16[4,512,16,64]{1,0,3,2:T(4,128)(2,1)} %reshape.111) | data formatting | bytes 8388608
  208.4 24.8 %all-gather.8.cloned.1.call-done = bf16[2048,1024]{1,0:T(8,128)(2,1)} async-done(((bf16[512,1024]{1,0:T(8,128)(2,1)}), bf16[2048,1024]{1,0:T(8,128)(2,1)}) %all-gather.8.cloned.1.call-update) | async-done | bytes 4194320 | tf_op jit(solution)/shard_map/all_gather | solution.py:100
  233.2 11.7 %reshape.112 = bf16[4,512,16,64]{3,2,1,0:T(8,128)(2,1)} reshape(bf16[2048,1024]{1,0:T(8,128)(2,1)} %all-gather.8.cloned.1.call-done) | data formatting | bytes 8388608 | tf_op jit(solution)/shard_map/reshape | solution.py:104
  245.0 9.7 %copy.34 = bf16[4,512,16,64]{1,3,2,0:T(8,128)(2,1)} copy(bf16[4,512,16,64]{3,2,1,0:T(8,128)(2,1)} %reshape.112) | data formatting | bytes 8388608
  254.7 104.7 %while.15 = (s32[]{:T(128)}, f32[16,512]{1,0:T(8,128)S(1)}, f32[16,512]{1,0:T(8,128)S(1)}, f32[512,16,64]{0,2,1:T(8,128)}, pred[512]{0:T(512)(128)(4,1)S(1)}, /*...) while((s32[]{:T(128)}, f32[16,512]{1,0:T(8,128)S(1)}, ...), condition=%wide.region_9.10_spmd.clone, body=%wide.region_6.9_spmd.clone.sunk | while | flops 1130151936 | bytes 126356832 | solution.py:107
  255.0 9.0 %fusion.58 = (f32[16,512]{1,0:T(8,128)S(1)}, f32[16,512,512]{2,1,0:T(8,128)}) fusion(f32[16]{0:T(128)S(1)} %get-tuple-element.252, pred[512,512]{0,1:T(8,128)(4,1)S(1)} %broadcast_compare_fusion.2, bf16[512,16,64]{0,2,1:T(8,128)(2,1)S(1)} %get-tuple-element.251, bf16[4,512,16,64]{1,3,2,0:T(8,128)(2,1)} %get-tuple-element.250, s32[]{:T(128)} %get-tuple-element.232), kind=kOutput, calls=%fused_computation.2.clone.1 | convolution fusion | flops 549445632 | bytes 19169856 | tf_op jit(solution)/shard_map/while/body/eval_jaxpr/ihd,jhd->hij/dot_general | solution.py:86
  264.0 12.5 %bitcast_add_fusion.2 = f32[512,16,64]{0,2,1:T(8,128)} fusion(f32[512,16,64]{0,2,1:T(8,128)} %get-tuple-element.235, f32[16,512,512]{2,1,0:T(8,128)} %get-tuple-element.218, f32[16,512]{1,0:T(8,128)S(1)} %get-tuple-element.245, f32[16]{0:T(128)S(1)} %get-tuple-element.252, pred[512,512]{0,1:T(8,128)(4,1)S(1)} %broadcast_compare_fusion.2, ...), kind=kOutput, calls=%fused_computation.7.clone.1 | convolution fusion | flops 559415296 | bytes 22348352 | tf_op jit(solution)/shard_map/while/body/eval_jaxpr/hij,jhd->ihd/dot_general | solution.py:94
  281.0 8.8 %fusion.58 = (f32[16,512]{1,0:T(8,128)S(1)}, f32[16,512,512]{2,1,0:T(8,128)}) fusion(f32[16]{0:T(128)S(1)} %get-tuple-element.252, pred[512,512]{0,1:T(8,128)(4,1)S(1)} %broadcast_compare_fusion.2, bf16[512,16,64]{0,2,1:T(8,128)(2,1)S(1)} %get-tuple-element.251, bf16[4,512,16,64]{1,3,2,0:T(8,128)(2,1)} %get-tuple-element.250, s32[]{:T(128)} %get-tuple-element.232), kind=kOutput, calls=%fused_computation.2.clone.1 | convolution fusion | flops 549445632 | bytes 19169856 | tf_op jit(solution)/shard_map/while/body/eval_jaxpr/ihd,jhd->hij/dot_general | solution.py:86
  289.8 12.9 %bitcast_add_fusion.2 = f32[512,16,64]{0,2,1:T(8,128)} fusion(f32[512,16,64]{0,2,1:T(8,128)} %get-tuple-element.235, f32[16,512,512]{2,1,0:T(8,128)} %get-tuple-element.218, f32[16,512]{1,0:T(8,128)S(1)} %get-tuple-element.245, f32[16]{0:T(128)S(1)} %get-tuple-element.252, pred[512,512]{0,1:T(8,128)(4,1)S(1)} %broadcast_compare_fusion.2, ...), kind=kOutput, calls=%fused_computation.7.clone.1 | convolution fusion | flops 559415296 | bytes 22348352 | tf_op jit(solution)/shard_map/while/body/eval_jaxpr/hij,jhd->ihd/dot_general | solution.py:94
  307.2 8.8 %fusion.58 = (f32[16,512]{1,0:T(8,128)S(1)}, f32[16,512,512]{2,1,0:T(8,128)}) fusion(f32[16]{0:T(128)S(1)} %get-tuple-element.252, pred[512,512]{0,1:T(8,128)(4,1)S(1)} %broadcast_compare_fusion.2, bf16[512,16,64]{0,2,1:T(8,128)(2,1)S(1)} %get-tuple-element.251, bf16[4,512,16,64]{1,3,2,0:T(8,128)(2,1)} %get-tuple-element.250, s32[]{:T(128)} %get-tuple-element.232), kind=kOutput, calls=%fused_computation.2.clone.1 | convolution fusion | flops 549445632 | bytes 19169856 | tf_op jit(solution)/shard_map/while/body/eval_jaxpr/ihd,jhd->hij/dot_general | solution.py:86
  316.1 12.9 %bitcast_add_fusion.2 = f32[512,16,64]{0,2,1:T(8,128)} fusion(f32[512,16,64]{0,2,1:T(8,128)} %get-tuple-element.235, f32[16,512,512]{2,1,0:T(8,128)} %get-tuple-element.218, f32[16,512]{1,0:T(8,128)S(1)} %get-tuple-element.245, f32[16]{0:T(128)S(1)} %get-tuple-element.252, pred[512,512]{0,1:T(8,128)(4,1)S(1)} %broadcast_compare_fusion.2, ...), kind=kOutput, calls=%fused_computation.7.clone.1 | convolution fusion | flops 559415296 | bytes 22348352 | tf_op jit(solution)/shard_map/while/body/eval_jaxpr/hij,jhd->ihd/dot_general | solution.py:94
  333.5 8.8 %fusion.58 = (f32[16,512]{1,0:T(8,128)S(1)}, f32[16,512,512]{2,1,0:T(8,128)}) fusion(f32[16]{0:T(128)S(1)} %get-tuple-element.252, pred[512,512]{0,1:T(8,128)(4,1)S(1)} %broadcast_compare_fusion.2, bf16[512,16,64]{0,2,1:T(8,128)(2,1)S(1)} %get-tuple-element.251, bf16[4,512,16,64]{1,3,2,0:T(8,128)(2,1)} %get-tuple-element.250, s32[]{:T(128)} %get-tuple-element.232), kind=kOutput, calls=%fused_computation.2.clone.1 | convolution fusion | flops 549445632 | bytes 19169856 | tf_op jit(solution)/shard_map/while/body/eval_jaxpr/ihd,jhd->hij/dot_general | solution.py:86
  342.3 12.9 %bitcast_add_fusion.2 = f32[512,16,64]{0,2,1:T(8,128)} fusion(f32[512,16,64]{0,2,1:T(8,128)} %get-tuple-element.235, f32[16,512,512]{2,1,0:T(8,128)} %get-tuple-element.218, f32[16,512]{1,0:T(8,128)S(1)} %get-tuple-element.245, f32[16]{0:T(128)S(1)} %get-tuple-element.252, pred[512,512]{0,1:T(8,128)(4,1)S(1)} %broadcast_compare_fusion.2, ...), kind=kOutput, calls=%fused_computation.7.clone.1 | convolution fusion | flops 559415296 | bytes 22348352 | tf_op jit(solution)/shard_map/while/body/eval_jaxpr/hij,jhd->ihd/dot_general | solution.py:94
  361.4 5.9 %fusion.24 = bf16[512,2048]{1,0:T(8,128)(2,1)} fusion(bf16[512,2048]{1,0:T(8,128)(2,1)S(1)} %copy-done.1, bf16[512,1024]{0,1:T(8,128)(2,1)S(1)} %bitcast.62, bf16[1024,2048]{1,0:T(8,128)(2,1)} %all-gather.14.cloned.1.call-done), kind=kOutput, calls=%fused_computation.33 | convolution fusion | flops 2150629376 | bytes 9437184 | tf_op jit(solution)/shard_map/dot_general | solution.py:111
  (91 shorter events, 60.6 us)
Async XLA Ops:
  6.5 4.2 %copy-start.1 = (bf16[512,2048]{1,0:T(8,128)(2,1)S(1)}, bf16[512,2048]{1,0:T(8,128)(2,1)}, u32[]{:S(2)}) copy-start(bf16[512,2048]{1,0:T(8,128)(2,1)} %param.11) | copy-start | bytes 6291460
  6.5 42.2 %copy-start.6 = (f32[2048]{0:T(1024)S(1)}, f32[2048]{0:T(1024)}, u32[]{:S(2)}) copy-start(f32[2048]{0:T(1024)} %param.14) | copy-start | bytes 24580
  6.5 42.2 %all-gather.6.cloned.1.call-start = ((), (), s32[]{:S(2)}) async-start(), calls=%async_computation | async-start | bytes 4718592 | tf_op jit(solution)/shard_map/all_gather | solution.py:64
  7.3 80.1 %all-gather.12.cloned.1.call-start = ((), (), s32[]{:S(2)}) async-start(), calls=%async_computation.3 | async-start | bytes 4718592 | tf_op jit(solution)/shard_map/all_gather | solution.py:65
  8.0 118.0 %all-gather.10.cloned.1.call-start = ((), (), s32[]{:S(2)}) async-start(), calls=%async_computation.2 | async-start | bytes 4718592 | tf_op jit(solution)/shard_map/all_gather | solution.py:63
  8.7 224.5 %all-gather.8.cloned.1.call-start = ((), (), s32[]{:S(2)}) async-start(), calls=%async_computation.1 | async-start | bytes 5242880 | tf_op jit(solution)/shard_map/all_gather | solution.py:100
  68.3 293.1 %all-gather.14.cloned.1.call-start = ((), (), s32[]{:S(2)}) async-start(), calls=%async_computation.4 | async-start | bytes 4718592 | tf_op jit(solution)/shard_map/all_gather | solution.py:113
  68.8 26.2 %copy-start.5 = (s32[1,4]{1,0:T(1,128)S(1)}, s32[1,4]{1,0:T(1,128)}, u32[]{:S(2)}) copy-start(s32[1,4]{1,0:T(1,128)} %param.12) | copy-start | bytes 52
  92.9 28.1 %collective-permute-start = (bf16[512,1024]{1,0:T(8,128)(2,1)}, bf16[512,1024]{1,0:T(8,128)(2,1)}, u32[]{:S(2)}, u32[]{:S(2)}) collective-permute-start(bf16[512,1024]{1,0:T(8,128)(2,1)} %convolution_convert_fusion), channel_id=1, source_target_pairs={{0,1},{1,2},{2,3},{3,0},{4,5},{5,6},{6,7},{7,4},{8,9},{9,10},{10,1... | collective-permute-start | bytes 3145736 | tf_op jit(solution)/shard_map/ppermute | solution.py:16
  95.3 59.3 %collective-permute-start.1 = (bf16[512,1024]{1,0:T(8,128)(2,1)}, bf16[512,1024]{1,0:T(8,128)(2,1)}, u32[]{:S(2)}, u32[]{:S(2)}) collective-permute-start(bf16[512,1024]{1,0:T(8,128)(2,1)} %convolution_convert_fusion), channel_id=1, source_target_pairs={{0,3},{1,0},{2,1},{3,2},{4,7},{5,4},{6,5},{7,6},{8,11},{9,8},{10,9... | collective-permute-start | bytes 3145736 | tf_op jit(solution)/shard_map/ppermute | solution.py:19
  121.1 69.8 %collective-permute-start.2 = (bf16[512,1024]{1,0:T(8,128)(2,1)}, bf16[512,1024]{1,0:T(8,128)(2,1)}, u32[]{:S(2)}, u32[]{:S(2)}) collective-permute-start(bf16[512,1024]{1,0:T(8,128)(2,1)} %collective-permute-done), channel_id=1, source_target_pairs={{0,1},{1,2},{2,3},{3,0},{4,5},{5,6},{6,7},{7,4},{8,9},{9,10},{10,1... | collective-permute-start | bytes 3145736 | tf_op jit(solution)/shard_map/ppermute | solution.py:16
  133.5 2.7 copy-start.3
  134.2 1.9 copy-start.2
  245.0 9.8 %copy-start.4 = (f32[16]{0:T(128)S(1)}, f32[16]{0:T(128)}, u32[]{:S(2)}) copy-start(f32[16]{0:T(128)} %param.19) | copy-start | bytes 196
  264.0 12.5 %copy-start = (f32[16,512,512]{2,1,0:T(8,128)S(1)}, f32[16,512,512]{2,1,0:T(8,128)}, u32[]{:S(2)}) copy-start(f32[16,512,512]{2,1,0:T(8,128)} %get-tuple-element.218) | copy-start | bytes 50331652 | tf_op jit(solution)/shard_map/while
  289.8 12.9 %copy-start = (f32[16,512,512]{2,1,0:T(8,128)S(1)}, f32[16,512,512]{2,1,0:T(8,128)}, u32[]{:S(2)}) copy-start(f32[16,512,512]{2,1,0:T(8,128)} %get-tuple-element.218) | copy-start | bytes 50331652 | tf_op jit(solution)/shard_map/while
  316.0 12.9 %copy-start = (f32[16,512,512]{2,1,0:T(8,128)S(1)}, f32[16,512,512]{2,1,0:T(8,128)}, u32[]{:S(2)}) copy-start(f32[16,512,512]{2,1,0:T(8,128)} %get-tuple-element.218) | copy-start | bytes 50331652 | tf_op jit(solution)/shard_map/while
  342.3 12.9 %copy-start = (f32[16,512,512]{2,1,0:T(8,128)S(1)}, f32[16,512,512]{2,1,0:T(8,128)}, u32[]{:S(2)}) copy-start(f32[16,512,512]{2,1,0:T(8,128)} %get-tuple-element.218) | copy-start | bytes 50331652 | tf_op jit(solution)/shard_map/while
Sparse Core Ops, SparseCore 0:
  9.2 39.4 all-gather.5
  50.6 36.7 all-gather.11
  89.2 36.7 all-gather.9
  127.4 105.7 all-gather.7
  235.0 34.7 all-gather.13
